TPU v7x, 32 devices: a whole 2x2x4 slice. The times are simulated.
32 devices in a mesh: cols: 8 (over z, x), rows: 4 (over y, core).
Axes of the slice: x: 2, y: 2, z: 4, core: 2. Of those that a mesh axis runs over, the one named last changes fastest.
Arguments:
- slide_pixels: bfloat16 [3, 1024, 4096], P(None, 'rows', 'cols'), may hold values from -6 to 6
- stem_first: bfloat16 [6, 6, 3, 64], replicated, may hold values from -0.625 to 0.625
- stem_second: bfloat16 [6, 6, 64, 256], replicated, may hold values from -0.125 to 0.125
- stem_third: bfloat16 [3, 3, 256, 1024], replicated, may hold values from -0.125 to 0.125
- key_weight: bfloat16 [1024, 1024], replicated, may hold values from -0.1875 to 0.1875
- value_weight: bfloat16 [1024, 1024], replicated, may hold values from -0.1875 to 0.1875
- queries: bfloat16 [512, 1024], replicated, may hold values from -240 to 240
Outputs:
- attended: bfloat16 [512, 1024], P(('cols', 'rows'))
All inputs are finite; a program needn't handle non-finite values.
Results may differ from a plain program's by a relative error of at most 0.033.
Values may be sent and summed in bfloat16 or wider, within the bound.
No kernel may reach another device: no remote copies, remote signals or barrier semaphores. Data moves between devices by JAX's collectives and lax.ppermute only.
A program may use at most 128 MiB of HBM per device.

v0:
```python
import math
import jax
import jax.numpy as jnp
from jax import lax
from jax.sharding import PartitionSpec as P

HEADS = 8


def with_halo(shard, sides, width):
    for axis, dim in sides:
        size, length = (lax.axis_size(axis), shard.shape[dim])
        up = [(i, (i + 1) % size) for i in range(size - 1)]
        down = [(j, i) for i, j in up]
        last = lax.slice_in_dim(shard, length - width, length, axis=dim)
        leading = lax.slice_in_dim(shard, 0, width, axis=dim)
        before = lax.ppermute(last, axis, up)
        after = lax.ppermute(leading, axis, down)
        shard = jnp.concatenate([before, shard, after], axis=dim)
    return shard


def shifted(value, axis, steps):
    count = lax.axis_size(axis)
    leading, last = (max(0, -steps), min(count, count - steps))
    return lax.ppermute(value, axis, [(source, source + steps) for source in range(leading, last)])


def extend(features):
    return with_halo(features, (("cols", 2), ("rows", 1)), 1)


def convolve(features, kernel, stride, layout):
    return lax.conv_general_dilated(
        features[None],
        kernel,
        (stride, stride),
        "VALID",
        dimension_numbers=layout,
        preferred_element_type=jnp.float32,
    )[0]


def norm_rows(features):
    tok_mean = jnp.mean(features, axis=-1, keepdims=True)
    centred = features - tok_mean
    tok_var = jnp.mean(centred * centred, axis=-1, keepdims=True)
    return (centred * lax.rsqrt(tok_var + 1e-05)).astype(jnp.bfloat16)


def on_device(slide_pixels, stem_first, stem_second, stem_third, key_weight, value_weight, queries):
    first_map = jax.nn.gelu(
        convolve(extend(slide_pixels), stem_first, 4, ("NCHW", "HWIO", "NCHW"))
    ).astype(jnp.bfloat16)
    second_map = jax.nn.gelu(
        convolve(extend(first_map), stem_second, 4, ("NCHW", "HWIO", "NHWC"))
    ).astype(jnp.bfloat16)
    upper_rim = shifted(second_map[-1:], "rows", 1)
    second_map = jnp.concatenate([upper_rim, second_map], axis=0)
    left_rim = shifted(second_map[:, -1:], "cols", 1)
    second_map = jnp.concatenate([left_rim, second_map], axis=1)
    third_map = convolve(second_map, stem_third, 2, ("NHWC", "HWIO", "NHWC"))
    model_width = third_map.shape[-1]
    normed = norm_rows(third_map.reshape(-1, model_width))
    tok_count = normed.shape[0]
    key_rows = jnp.dot(normed, key_weight, preferred_element_type=jnp.float32).astype(jnp.bfloat16)
    value_rows = jnp.dot(normed, value_weight, preferred_element_type=jnp.float32).astype(
        jnp.bfloat16
    )
    head_size = model_width // HEADS
    latent_count = queries.shape[0]
    query_heads = queries.reshape(latent_count, HEADS, head_size)
    scores = jnp.einsum(
        "lhd,thd->hlt",
        query_heads,
        key_rows.reshape(tok_count, HEADS, head_size),
        preferred_element_type=jnp.float32,
    ) * (1.0 / math.sqrt(head_size))
    peak_score = lax.pmax(jnp.max(scores, axis=2), ("cols", "rows"))
    weights = jnp.exp(scores - peak_score[:, :, None])
    row_total = jnp.sum(weights, axis=2).T
    rounded = weights.astype(jnp.bfloat16)
    weighted = jnp.einsum(
        "hlt,thd->lhd",
        rounded,
        value_rows.reshape(tok_count, HEADS, head_size),
        preferred_element_type=jnp.float32,
    ).reshape(latent_count, model_width)
    share_rows = latent_count // lax.axis_size(("cols", "rows"))
    weighted, row_total = lax.psum((weighted, row_total), ("cols", "rows"))
    share_start = lax.axis_index(("cols", "rows")) * share_rows
    weighted = lax.dynamic_slice_in_dim(weighted, share_start, share_rows, 0)
    row_total = lax.dynamic_slice_in_dim(row_total, share_start, share_rows, 0)
    attended = weighted.reshape(share_rows, HEADS, head_size) / row_total[:, :, None]
    return attended.reshape(share_rows, model_width).astype(jnp.bfloat16)


def solution(mesh):
    placed = (P(None, "rows", "cols"), P(), P(), P(), P(), P(), P())
    return jax.shard_map(
        on_device, mesh=mesh, in_specs=placed, out_specs=P(("cols", "rows"), None), check_vma=False
    )
```

profile of v0, /device:TPU:0, one launch (start us, length us, event | category | flops | bytes accessed | tf_op | source)
XLA Modules:
  0.0 329.5 jit_solution(13825358691176323215)
XLA Ops:
  6.5 1.3 fusion.73
  7.8 4.9 %collective-permute-start = (bf16[3,256,1]{2,1,0:T(8,128)(2,1)S(1)}, bf16[3,256,1]{2,1,0:T(8,128)(2,1)S(1)}, u32[]{:S(2)}, u32[]{:S(2)}) collective-permute-start(bf16[3,256,1]{2,1,0:T(8,128)(2,1)S(1)} %get-tuple-element.13), channel_id=1, source_target_pairs={{0,4},{4,8},{8,12},{12,16},{16,20},{20,24},{24,28},{1,5},{5,9},{9,... | collective-permute-start | bytes 4616 | tf_op jit(solution)/shard_map/ppermute | solution.py:17
  12.7 1.3 collective-permute-start.1
  14.0 2.9 collective-permute-done
  16.9 4.0 %collective-permute-done.1 = bf16[3,256,1]{2,1,0:T(8,128)(2,1)S(1)} collective-permute-done((bf16[3,256,1]{2,1,0:T(8,128)(2,1)S(1)}, bf16[3,256,1]{2,1,0:T(8,128)(2,1)S(1)}, u32[]{:S(2)}, u32[]{:S(2)}) %collective-permute-start.1) | collective-permute-done | bytes 1568 | tf_op jit(solution)/shard_map/ppermute | solution.py:18
  21.0 0.8 pad_maximum_fusion.6
  21.8 1.3 collective-permute-start.2
  23.1 1.3 collective-permute-start.3
  24.4 3.5 %collective-permute-done.3 = bf16[3,1,514]{2,1,0:T(2,128)(2,1)S(1)} collective-permute-done((bf16[3,1,514]{2,1,0:T(2,128)(2,1)S(1)}, bf16[3,1,514]{2,1,0:T(2,128)(2,1)S(1)}, u32[]{:S(2)}, u32[]{:S(2)}) %collective-permute-start.3) | collective-permute-done | bytes 3116 | tf_op jit(solution)/shard_map/ppermute | solution.py:18
  27.9 0.9 maximum_bitcast_fusion.1
  28.9 2.8 reshape.95
  31.7 19.5 %copy.95 = bf16[3,258,1,8,68]{3,0,4,1,2:T(4,128)(2,1)} copy(bf16[3,258,1,8,68]{4,3,1,0,2:T(8,128)(2,1)} %reshape.95) | data formatting | bytes 1684224 | tf_op jit(solution)/shard_map/conv_general_dilated | solution.py:34
  51.1 2.1 slice.46
  53.3 23.5 %broadcast_select_fusion = f32[64,8,17,64]{3,1,2,0:T(8,128)S(1)} fusion(pred[8,17]{0,1:T(8,128)(4,1)S(1)} %copy-done.5, bf16[6,6,3,64]{3,2,1,0:T(4,128)(2,1)S(1)} %copy-done.4, bf16[3,258,1,7,5]{3,0,4,1,2:T(4,128)(2,1)S(1)} %slice.46, bf16[3,258,1,8,68]{3,0,4,1,2:T(4,128)(2,1)} %copy.95), kind=kOutput, calls=%fused_computation.25 | convolution fusion | flops 123593248 | bytes 3138476 | tf_op jit(solution)/shard_map/conv_general_dilated | solution.py:34
  76.8 0.9 copy.96
  77.6 1.4 fusion.14
  79.0 4.5 %collective-permute-start.4 = (bf16[64,64,1]{0,1,2:T(8,128)(2,1)S(1)}, bf16[64,64,1]{0,1,2:T(8,128)(2,1)S(1)}, u32[]{:S(2)}, u32[]{:S(2)}) collective-permute-start(bf16[64,64,1]{0,1,2:T(8,128)(2,1)S(1)} %get-tuple-element.7), channel_id=1, source_target_pairs={{0,4},{4,8},{8,12},{12,16},{16,20},{20,24},{24,28},{1,5},{5,9},{9,... | collective-permute-start | bytes 24584 | tf_op jit(solution)/shard_map/ppermute | solution.py:17
  83.5 1.3 collective-permute-start.5
  84.9 4.6 %collective-permute-done.5 = bf16[64,64,1]{0,1,2:T(8,128)(2,1)S(1)} collective-permute-done((bf16[64,64,1]{0,1,2:T(8,128)(2,1)S(1)}, bf16[64,64,1]{0,1,2:T(8,128)(2,1)S(1)}, u32[]{:S(2)}, u32[]{:S(2)}) %collective-permute-start.5) | collective-permute-done | bytes 8224 | tf_op jit(solution)/shard_map/ppermute | solution.py:18
  89.7 3.2 collective-permute-start.6
  92.9 1.5 collective-permute-start.7
  94.4 2.3 collective-permute-done.7
  96.7 4.0 %maximum_bitcast_fusion = bf16[64,66,1,130]{0,1,3,2:T(8,128)(2,1)} fusion(bf16[64,1,130]{0,1,2:T(2,128)(2,1)S(1)} %collective-permute-done.7, bf16[64,64,1]{0,1,2:T(8,128)(2,1)S(1)} %collective-permute-done.5, bf16[64,64,128]{0,1,2:T(8,128)(2,1)S(1)} %fusion.14, bf16[64,64,1]{0,1,2:T(8,128)(2,1)S(1)} %collective-permute-done.4, ...), kind=kLoop, calls=%fused_computation.24 | loop fusion | flops 5491200 | bytes 2196480 | tf_op jit(solution)/shard_map/broadcast_in_dim | solution.py:35
  100.7 4.4 %copy.122 = bf16[64,66,1,130]{1,0,3,2:T(8,128)(2,1)} copy(bf16[64,66,1,130]{0,1,3,2:T(8,128)(2,1)} %maximum_bitcast_fusion) | data formatting | bytes 2196480
  105.0 3.9 %pad.2.clone = bf16[64,66,1,160]{1,0,3,2:T(8,128)(2,1)} pad(bf16[64,66,1,130]{1,0,3,2:T(8,128)(2,1)} %copy.122, bf16[]{:T(256)} %constant.41), padding=0_0x0_0x0_0x0_30 | pad | bytes 2449922 | tf_op jit(solution)/shard_map/broadcast_in_dim | solution.py:35
  108.9 4.9 %copy.99 = bf16[64,66,1,8,20]{0,3,4,1,2:T(8,128)(2,1)} copy(bf16[64,66,1,8,20]{1,0,4,3,2:T(8,128)(2,1)} %bitcast.93) | data formatting | bytes 2703360 | tf_op jit(solution)/shard_map/conv_general_dilated | solution.py:34
  113.8 1.4 slice.50
  115.3 3.0 fusion.28
  118.2 0.2 copy.100
  118.7 4.8 %collective-permute-start.8 = (bf16[1,32,256]{2,0,1:T(2,128)(2,1)S(1)}, bf16[1,32,256]{2,0,1:T(2,128)(2,1)S(1)}, u32[]{:S(2)}, u32[]{:S(2)}) collective-permute-start(bf16[1,32,256]{2,0,1:T(2,128)(2,1)S(1)} %slice.52), channel_id=1, source_target_pairs={{0,1},{1,2},{2,3},{4,5},{5,6},{6,7},{8,9},{9,10},{10,11},{12,13},{... | collective-permute-start | bytes 49160 | tf_op jit(solution)/shard_map/ppermute | solution.py:26
  123.6 0.8 collective-permute-done.8
  124.4 4.8 %collective-permute-start.9 = (bf16[17,1,256]{2,0,1:T(8,128)(2,1)S(1)}, bf16[17,1,256]{2,0,1:T(8,128)(2,1)S(1)}, u32[]{:S(2)}, u32[]{:S(2)}) collective-permute-start(bf16[17,1,256]{2,0,1:T(8,128)(2,1)S(1)} %pad_maximum_fusion.3), channel_id=1, source_target_pairs={{0,4},{4,8},{8,12},{12,16},{16,20},{20,24},{24,28},{1,5},{5,9},{9,... | collective-permute-start | bytes 26120 | tf_op jit(solution)/shard_map/ppermute | solution.py:26
  129.2 1.4 collective-permute-done.9
  131.0 1.1 convolution_select_fusion
  132.2 0.5 copy.104
  133.0 0.2 fusion.55
  133.4 0.3 copy.105
  133.8 0.4 fusion.31
  134.3 0.3 copy-done.2
  134.6 1.8 bitcast_reduce_fusion
  136.4 42.2 %pmax.7 = f32[8,512]{1,0:T(8,128)S(1)} all-reduce(f32[8,512]{1,0:T(8,128)S(1)} %get-tuple-element.15), channel_id=1, replica_groups=mesh['cols'=8,'rows'=4] {'cols','rows'}, use_global_device_ids=true, to_apply=%region_3.0 | all-reduce | flops 4096 | bytes 32768 | tf_op jit(solution)/shard_map/pmax | solution.py:79
  178.6 2.0 convolution_convert_fusion.1
  180.8 3.4 %fusion.33 = f32[8,128,512]{2,1,0:T(8,128)} fusion(bf16[128,8,128]{0,2,1:T(8,128)(2,1)S(1)} %bitcast.99, f32[8,128,512]{2,1,0:T(8,128)} %get-tuple-element.16, f32[8,512]{1,0:T(8,128)S(1)} %pmax.7), kind=kOutput, calls=%fused_computation.39 | convolution fusion | flops 135790592 | bytes 4472832 | tf_op jit(solution)/shard_map/hlt,thd->lhd/dot_general | solution.py:83
  184.2 2.9 copy.113
  187.2 2.0 fusion.25
  189.1 40.1 %psum.15 = f32[512,8]{0,1:T(8,128)S(1)} all-reduce(f32[512,8]{0,1:T(8,128)S(1)} %bitcast.101), channel_id=1, replica_groups=mesh['cols'=8,'rows'=4] {'cols','rows'}, use_global_device_ids=true, to_apply=%region_6.0 | all-reduce | flops 4096 | bytes 32768 | tf_op jit(solution)/shard_map/psum | solution.py:90
  229.4 91.8 %all-reduce.2.cloned.1.call-done = f32[512,1024]{1,0:T(8,128)} async-done(((f32[512,1024]{1,0:T(8,128)}), f32[512,1024]{1,0:T(8,128)}) %all-reduce.2.cloned.1.call-update) | async-done | bytes 2097168 | tf_op jit(solution)/shard_map/psum | solution.py:90
  321.2 1.5 fusion.61
  (48 shorter events, 2.0 us)
Async XLA Ops:
  6.5 127.3 %copy-start = (bf16[1024,1024]{1,0:T(8,128)(2,1)S(1)}, bf16[1024,1024]{1,0:T(8,128)(2,1)}, u32[]{:S(2)}) copy-start(bf16[1024,1024]{1,0:T(8,128)(2,1)} %param.11) | copy-start | bytes 6291460
  6.5 21.4 %copy-start.1 = (bf16[3,256,512]{2,1,0:T(8,128)(2,1)S(1)}, bf16[3,256,512]{2,1,0:T(8,128)(2,1)}, u32[]{:S(2)}) copy-start(bf16[3,256,512]{2,1,0:T(8,128)(2,1)} %param.7) | copy-start | bytes 2359300
  6.5 314.6 %all-reduce.2.cloned.1.call-start = ((), (), s32[]{:S(2)}) async-start(), calls=%async_computation | async-start | bytes 4194304 | tf_op jit(solution)/shard_map/psum | solution.py:90
  7.8 9.1 %collective-permute-start = (bf16[3,256,1]{2,1,0:T(8,128)(2,1)S(1)}, bf16[3,256,1]{2,1,0:T(8,128)(2,1)S(1)}, u32[]{:S(2)}, u32[]{:S(2)}) collective-permute-start(bf16[3,256,1]{2,1,0:T(8,128)(2,1)S(1)} %get-tuple-element.13), channel_id=1, source_target_pairs={{0,4},{4,8},{8,12},{12,16},{16,20},{20,24},{24,28},{1,5},{5,9},{9,... | collective-permute-start | bytes 4616 | tf_op jit(solution)/shard_map/ppermute | solution.py:17
  12.7 8.3 %collective-permute-start.1 = (bf16[3,256,1]{2,1,0:T(8,128)(2,1)S(1)}, bf16[3,256,1]{2,1,0:T(8,128)(2,1)S(1)}, u32[]{:S(2)}, u32[]{:S(2)}) collective-permute-start(bf16[3,256,1]{2,1,0:T(8,128)(2,1)S(1)} %get-tuple-element.14), channel_id=1, source_target_pairs={{4,0},{8,4},{12,8},{16,12},{20,16},{24,20},{28,24},{5,1},{9,5},{13... | collective-permute-start | bytes 4616 | tf_op jit(solution)/shard_map/ppermute | solution.py:18
  21.8 2.6 collective-permute-start.2
  23.1 4.8 %collective-permute-start.3 = (bf16[3,1,514]{2,1,0:T(2,128)(2,1)S(1)}, bf16[3,1,514]{2,1,0:T(2,128)(2,1)S(1)}, u32[]{:S(2)}, u32[]{:S(2)}) collective-permute-start(bf16[3,1,514]{2,1,0:T(2,128)(2,1)S(1)} %get-tuple-element.10), channel_id=1, source_target_pairs={{1,0},{2,1},{3,2},{5,4},{6,5},{7,6},{9,8},{10,9},{11,10},{13,12},{... | collective-permute-start | bytes 9260 | tf_op jit(solution)/shard_map/ppermute | solution.py:18
  51.1 2.1 copy-start.4
  51.1 2.1 copy-start.5
  79.0 5.9 %collective-permute-start.4 = (bf16[64,64,1]{0,1,2:T(8,128)(2,1)S(1)}, bf16[64,64,1]{0,1,2:T(8,128)(2,1)S(1)}, u32[]{:S(2)}, u32[]{:S(2)}) collective-permute-start(bf16[64,64,1]{0,1,2:T(8,128)(2,1)S(1)} %get-tuple-element.7), channel_id=1, source_target_pairs={{0,4},{4,8},{8,12},{12,16},{16,20},{20,24},{24,28},{1,5},{5,9},{9,... | collective-permute-start | bytes 24584 | tf_op jit(solution)/shard_map/ppermute | solution.py:17
  83.5 6.1 %collective-permute-start.5 = (bf16[64,64,1]{0,1,2:T(8,128)(2,1)S(1)}, bf16[64,64,1]{0,1,2:T(8,128)(2,1)S(1)}, u32[]{:S(2)}, u32[]{:S(2)}) collective-permute-start(bf16[64,64,1]{0,1,2:T(8,128)(2,1)S(1)} %get-tuple-element.8), channel_id=1, source_target_pairs={{4,0},{8,4},{12,8},{16,12},{20,16},{24,20},{28,24},{5,1},{9,5},{13... | collective-permute-start | bytes 24584 | tf_op jit(solution)/shard_map/ppermute | solution.py:18
  89.7 4.6 %collective-permute-start.6 = (bf16[64,1,130]{0,1,2:T(2,128)(2,1)S(1)}, bf16[64,1,130]{0,1,2:T(2,128)(2,1)S(1)}, u32[]{:S(2)}, u32[]{:S(2)}) collective-permute-start(bf16[64,1,130]{0,1,2:T(2,128)(2,1)S(1)} %get-tuple-element.5), channel_id=1, source_target_pairs={{0,1},{1,2},{2,3},{4,5},{5,6},{6,7},{8,9},{9,10},{10,11},{12,13},{... | collective-permute-start | bytes 49928 | tf_op jit(solution)/shard_map/ppermute | solution.py:17
  92.9 3.8 %collective-permute-start.7 = (bf16[64,1,130]{0,1,2:T(2,128)(2,1)S(1)}, bf16[64,1,130]{0,1,2:T(2,128)(2,1)S(1)}, u32[]{:S(2)}, u32[]{:S(2)}) collective-permute-start(bf16[64,1,130]{0,1,2:T(2,128)(2,1)S(1)} %get-tuple-element.6), channel_id=1, source_target_pairs={{1,0},{2,1},{3,2},{5,4},{6,5},{7,6},{9,8},{10,9},{11,10},{13,12},{... | collective-permute-start | bytes 49928 | tf_op jit(solution)/shard_map/ppermute | solution.py:18
  108.9 6.3 %copy-start.3 = (bf16[6,6,64,256]{3,2,1,0:T(8,128)(2,1)S(1)}, bf16[6,6,64,256]{3,2,1,0:T(8,128)(2,1)}, u32[]{:S(2)}) copy-start(bf16[6,6,64,256]{3,2,1,0:T(8,128)(2,1)} %param.9) | copy-start | bytes 3538948
  108.9 6.3 %copy-start.6 = (pred[8,5]{0,1:T(8,128)(4,1)S(1)}, pred[8,5]{0,1:T(8,128)(4,1)}, u32[]{:S(2)}) copy-start(pred[8,5]{0,1:T(8,128)(4,1)} %constant.54) | copy-start | bytes 124
  113.8 17.2 %slice-start = ((s8[4718592]{0:T(1024)(128)(4,1)}), s8[4194304]{0:T(1024)(128)(4,1)S(1)}, s32[]{:S(2)}) async-start(s8[4718592]{0:T(1024)(128)(4,1)} %bitcast.102), calls=%async_computation.1 | async-start | bytes 8388608
  115.3 15.8 %slice-start.1 = ((s8[4718592]{0:T(1024)(128)(4,1)}), s8[524288]{0:T(1024)(128)(4,1)S(1)}, s32[]{:S(2)}) async-start(s8[4718592]{0:T(1024)(128)(4,1)} %bitcast.102), calls=%async_computation.2 | async-start | bytes 1048576
  118.5 12.6 %copy-start.7 = (pred[8,3]{0,1:T(4,128)(4,1)S(1)}, pred[8,3]{0,1:T(4,128)(4,1)}, u32[]{:S(2)}) copy-start(pred[8,3]{0,1:T(4,128)(4,1)} %constant.53) | copy-start | bytes 76
  118.7 5.7 %collective-permute-start.8 = (bf16[1,32,256]{2,0,1:T(2,128)(2,1)S(1)}, bf16[1,32,256]{2,0,1:T(2,128)(2,1)S(1)}, u32[]{:S(2)}, u32[]{:S(2)}) collective-permute-start(bf16[1,32,256]{2,0,1:T(2,128)(2,1)S(1)} %slice.52), channel_id=1, source_target_pairs={{0,1},{1,2},{2,3},{4,5},{5,6},{6,7},{8,9},{9,10},{10,11},{12,13},{... | collective-permute-start | bytes 49160 | tf_op jit(solution)/shard_map/ppermute | solution.py:26
  124.4 6.2 %collective-permute-start.9 = (bf16[17,1,256]{2,0,1:T(8,128)(2,1)S(1)}, bf16[17,1,256]{2,0,1:T(8,128)(2,1)S(1)}, u32[]{:S(2)}, u32[]{:S(2)}) collective-permute-start(bf16[17,1,256]{2,0,1:T(8,128)(2,1)S(1)} %pad_maximum_fusion.3), channel_id=1, source_target_pairs={{0,4},{4,8},{8,12},{12,16},{16,20},{20,24},{24,28},{1,5},{5,9},{9,... | collective-permute-start | bytes 26120 | tf_op jit(solution)/shard_map/ppermute | solution.py:26
  133.4 1.2 copy-start.2
Sparse Core Ops, SparseCore 0:
  187.3 133.8 all-reduce.1
where the time goes:
time: 332 us; the launch traced here: 330 us
  waiting for transfers between devices  112 us (34%)
  blocking collectives  82.2 us (25%)
  local copies, waits for them, and re-layouts  46.4 us (14%)
  matrix products  35.3 us (11%)
  starting transfers between devices  28.8 us (9%)
  between operations  13.8 us (4%)
  other arithmetic  11.4 us (3%)
    psum x1, waiting for transfers between devices, on_device(): weighted, row_total = lax.psum((weighted, row_total), ('cols', 'rows'))  91.8 us
    pmax x1, blocking collectives, on_device(): peak_score = lax.pmax(jnp.max(scores, axis=2), ('cols', 'rows'))  42.2 us
    psum x1, blocking collectives, on_device(): weighted, row_total = lax.psum((weighted, row_total), ('cols', 'rows'))  40.1 us
    conv_general_dilated x11, local copies, waits for them, and re-layouts, convolve(): lax.conv_general_dilated(features[None], kernel, (stride, stride), 'VALID...  32.7 us
    conv_general_dilated x3, matrix products, convolve(): lax.conv_general_dilated(features[None], kernel, (stride, stride), 'VALID...  27.6 us
    ppermute x4, waiting for transfers between devices, with_halo(): after = lax.ppermute(leading, axis, down)  14.5 us
    ppermute x4, starting transfers between devices, with_halo(): before = lax.ppermute(last, axis, up)  13.8 us
    ppermute x2, starting transfers between devices, shifted(): lax.ppermute(value, axis, [(source, source + steps) for source in range(l...  9.66 us
  transfers between devices with their start and end apart: 11, of which 9 were waited for; matrix products, arithmetic and copies ran while one was open for 1% of the time, Pallas kernels for 0%

commit v1 on v0

--- a/solution.py
+++ b/solution.py
@@ -87,7 +87,7 @@
         preferred_element_type=jnp.float32,
     ).reshape(latent_count, model_width)
     share_rows = latent_count // lax.axis_size(("cols", "rows"))
-    weighted, row_total = lax.psum((weighted, row_total), ("cols", "rows"))
+    weighted, row_total = lax.psum(lax.psum((weighted, row_total), "rows"), "cols")
     share_start = lax.axis_index(("cols", "rows")) * share_rows
     weighted = lax.dynamic_slice_in_dim(weighted, share_start, share_rows, 0)
     row_total = lax.dynamic_slice_in_dim(row_total, share_start, share_rows, 0)

time: 332 us -> 356 us (1.072)
  waiting for transfers between devices: 112 us -> 127 us
  blocking collectives: 82.2 us -> 91 us
    psum x1 -> x2, waiting for transfers between devices: 91.8 us -> 107 us  [the longest x1 55.5 us: on_device(): lax.psum(lax.psum((weighted, row_total), 'rows'), 'cols')]
    psum x1 -> x2, blocking collectives: 40.1 us -> 48.8 us  [the longest x1 38.7 us: on_device(): lax.psum(lax.psum((weighted, row_total), 'rows'), 'cols')]
  transfers between devices with their start and end apart: 11 -> 12, of which waited for: 9 -> 10; matrix products, arithmetic and copies ran while one was open for 1% -> 1% of each run, Pallas kernels for 0% -> 0%
where the time goes in v1:
time: 356 us; the launch traced here: 353 us
  waiting for transfers between devices  127 us (36%)
  blocking collectives  91 us (26%)
  local copies, waits for them, and re-layouts  46.5 us (13%)
  matrix products  35.3 us (10%)
  starting transfers between devices  28.8 us (8%)
  between operations  13.8 us (4%)
  other arithmetic  11.4 us (3%)
    psum x1, waiting for transfers between devices, on_device(): lax.psum(lax.psum((weighted, row_total), 'rows'), 'cols')  55.5 us
    psum x1, waiting for transfers between devices, on_device(): lax.psum((weighted, row_total), 'rows')  51.3 us
    pmax x1, blocking collectives, on_device(): peak_score = lax.pmax(jnp.max(scores, axis=2), ('cols', 'rows'))  42.2 us
    psum x1, blocking collectives, on_device(): lax.psum(lax.psum((weighted, row_total), 'rows'), 'cols')  38.7 us
    conv_general_dilated x11, local copies, waits for them, and re-layouts, convolve(): lax.conv_general_dilated(features[None], kernel, (stride, stride), 'VALID...  32.8 us
    conv_general_dilated x3, matrix products, convolve(): lax.conv_general_dilated(features[None], kernel, (stride, stride), 'VALID...  27.6 us
    ppermute x4, waiting for transfers between devices, with_halo(): after = lax.ppermute(leading, axis, down)  14.5 us
    ppermute x4, starting transfers between devices, with_halo(): before = lax.ppermute(last, axis, up)  13.8 us
  transfers between devices with their start and end apart: 12, of which 10 were waited for; matrix products, arithmetic and copies ran while one was open for 1% of the time, Pallas kernels for 0%

profile of v1, /device:TPU:0, one launch (start us, length us, event | category | flops | bytes accessed | tf_op | source)
XLA Modules:
  0.0 353.4 jit_solution(13511896727431513970)
XLA Ops:
  6.5 1.3 fusion.73
  7.8 4.9 %collective-permute-start = (bf16[3,256,1]{2,1,0:T(8,128)(2,1)S(1)}, bf16[3,256,1]{2,1,0:T(8,128)(2,1)S(1)}, u32[]{:S(2)}, u32[]{:S(2)}) collective-permute-start(bf16[3,256,1]{2,1,0:T(8,128)(2,1)S(1)} %get-tuple-element.13), channel_id=1, source_target_pairs={{0,4},{4,8},{8,12},{12,16},{16,20},{20,24},{24,28},{1,5},{5,9},{9,... | collective-permute-start | bytes 4616 | tf_op jit(solution)/shard_map/ppermute | solution.py:17
  12.7 1.3 collective-permute-start.1
  14.0 2.9 collective-permute-done
  16.9 4.0 %collective-permute-done.1 = bf16[3,256,1]{2,1,0:T(8,128)(2,1)S(1)} collective-permute-done((bf16[3,256,1]{2,1,0:T(8,128)(2,1)S(1)}, bf16[3,256,1]{2,1,0:T(8,128)(2,1)S(1)}, u32[]{:S(2)}, u32[]{:S(2)}) %collective-permute-start.1) | collective-permute-done | bytes 1568 | tf_op jit(solution)/shard_map/ppermute | solution.py:18
  21.0 0.8 pad_maximum_fusion.6
  21.8 1.3 collective-permute-start.2
  23.1 1.3 collective-permute-start.3
  24.4 3.5 collective-permute-done.3
  27.9 0.9 maximum_bitcast_fusion.1
  28.9 2.8 reshape.95
  31.7 19.5 %copy.95 = bf16[3,258,1,8,68]{3,0,4,1,2:T(4,128)(2,1)} copy(bf16[3,258,1,8,68]{4,3,1,0,2:T(8,128)(2,1)} %reshape.95) | data formatting | bytes 1684224 | tf_op jit(solution)/shard_map/conv_general_dilated | solution.py:34
  51.2 2.1 slice.46
  53.3 23.5 %broadcast_select_fusion = f32[64,8,17,64]{3,1,2,0:T(8,128)S(1)} fusion(pred[8,17]{0,1:T(8,128)(4,1)S(1)} %copy-done.5, bf16[6,6,3,64]{3,2,1,0:T(4,128)(2,1)S(1)} %copy-done.4, bf16[3,258,1,7,5]{3,0,4,1,2:T(4,128)(2,1)S(1)} %slice.46, bf16[3,258,1,8,68]{3,0,4,1,2:T(4,128)(2,1)} %copy.95), kind=kOutput, calls=%fused_computation.25 | convolution fusion | flops 123593248 | bytes 3138476 | tf_op jit(solution)/shard_map/conv_general_dilated | solution.py:34
  76.8 0.9 copy.96
  77.7 1.4 fusion.14
  79.0 4.5 %collective-permute-start.4 = (bf16[64,64,1]{0,1,2:T(8,128)(2,1)S(1)}, bf16[64,64,1]{0,1,2:T(8,128)(2,1)S(1)}, u32[]{:S(2)}, u32[]{:S(2)}) collective-permute-start(bf16[64,64,1]{0,1,2:T(8,128)(2,1)S(1)} %get-tuple-element.7), channel_id=1, source_target_pairs={{0,4},{4,8},{8,12},{12,16},{16,20},{20,24},{24,28},{1,5},{5,9},{9,... | collective-permute-start | bytes 24584 | tf_op jit(solution)/shard_map/ppermute | solution.py:17
  83.5 1.3 collective-permute-start.5
  85.0 4.6 %collective-permute-done.5 = bf16[64,64,1]{0,1,2:T(8,128)(2,1)S(1)} collective-permute-done((bf16[64,64,1]{0,1,2:T(8,128)(2,1)S(1)}, bf16[64,64,1]{0,1,2:T(8,128)(2,1)S(1)}, u32[]{:S(2)}, u32[]{:S(2)}) %collective-permute-start.5) | collective-permute-done | bytes 8224 | tf_op jit(solution)/shard_map/ppermute | solution.py:18
  89.7 3.2 collective-permute-start.6
  92.9 1.5 collective-permute-start.7
  94.4 2.3 collective-permute-done.7
  96.7 4.0 %maximum_bitcast_fusion = bf16[64,66,1,130]{0,1,3,2:T(8,128)(2,1)} fusion(bf16[64,1,130]{0,1,2:T(2,128)(2,1)S(1)} %collective-permute-done.7, bf16[64,64,1]{0,1,2:T(8,128)(2,1)S(1)} %collective-permute-done.5, bf16[64,64,128]{0,1,2:T(8,128)(2,1)S(1)} %fusion.14, bf16[64,64,1]{0,1,2:T(8,128)(2,1)S(1)} %collective-permute-done.4, ...), kind=kLoop, calls=%fused_computation.24 | loop fusion | flops 5491200 | bytes 2196480 | tf_op jit(solution)/shard_map/broadcast_in_dim | solution.py:35
  100.7 4.3 %copy.122 = bf16[64,66,1,130]{1,0,3,2:T(8,128)(2,1)} copy(bf16[64,66,1,130]{0,1,3,2:T(8,128)(2,1)} %maximum_bitcast_fusion) | data formatting | bytes 2196480
  105.1 3.9 %pad.2.clone = bf16[64,66,1,160]{1,0,3,2:T(8,128)(2,1)} pad(bf16[64,66,1,130]{1,0,3,2:T(8,128)(2,1)} %copy.122, bf16[]{:T(256)} %constant.41), padding=0_0x0_0x0_0x0_30 | pad | bytes 2449922 | tf_op jit(solution)/shard_map/broadcast_in_dim | solution.py:35
  108.9 4.9 %copy.99 = bf16[64,66,1,8,20]{0,3,4,1,2:T(8,128)(2,1)} copy(bf16[64,66,1,8,20]{1,0,4,3,2:T(8,128)(2,1)} %bitcast.93) | data formatting | bytes 2703360 | tf_op jit(solution)/shard_map/conv_general_dilated | solution.py:34
  113.8 1.4 slice.50
  115.3 3.0 fusion.28
  118.7 4.8 %collective-permute-start.8 = (bf16[1,32,256]{2,0,1:T(2,128)(2,1)S(1)}, bf16[1,32,256]{2,0,1:T(2,128)(2,1)S(1)}, u32[]{:S(2)}, u32[]{:S(2)}) collective-permute-start(bf16[1,32,256]{2,0,1:T(2,128)(2,1)S(1)} %slice.52), channel_id=1, source_target_pairs={{0,1},{1,2},{2,3},{4,5},{5,6},{6,7},{8,9},{9,10},{10,11},{12,13},{... | collective-permute-start | bytes 49160 | tf_op jit(solution)/shard_map/ppermute | solution.py:26
  123.6 0.8 collective-permute-done.8
  124.4 4.8 %collective-permute-start.9 = (bf16[17,1,256]{2,0,1:T(8,128)(2,1)S(1)}, bf16[17,1,256]{2,0,1:T(8,128)(2,1)S(1)}, u32[]{:S(2)}, u32[]{:S(2)}) collective-permute-start(bf16[17,1,256]{2,0,1:T(8,128)(2,1)S(1)} %pad_maximum_fusion.3), channel_id=1, source_target_pairs={{0,4},{4,8},{8,12},{12,16},{16,20},{20,24},{24,28},{1,5},{5,9},{9,... | collective-permute-start | bytes 26120 | tf_op jit(solution)/shard_map/ppermute | solution.py:26
  129.3 1.4 collective-permute-done.9
  131.1 1.1 convolution_select_fusion
  132.2 0.5 copy.104
  133.4 0.3 copy.105
  133.9 0.4 fusion.31
  134.3 0.3 copy-done.2
  134.7 1.8 bitcast_reduce_fusion
  136.5 42.2 %pmax.7 = f32[8,512]{1,0:T(8,128)S(1)} all-reduce(f32[8,512]{1,0:T(8,128)S(1)} %get-tuple-element.15), channel_id=1, replica_groups=mesh['cols'=8,'rows'=4] {'cols','rows'}, use_global_device_ids=true, to_apply=%region_3.0 | all-reduce | flops 4096 | bytes 32768 | tf_op jit(solution)/shard_map/pmax | solution.py:79
  178.6 2.0 convolution_convert_fusion.1
  180.9 3.4 fusion.33
  184.3 2.9 copy.113
  187.3 51.3 %all-reduce.3.cloned.1.call-done = f32[512,1024]{1,0:T(8,128)} async-done(((f32[512,1024]{1,0:T(8,128)}), f32[512,1024]{1,0:T(8,128)}) %all-reduce.3.cloned.1.call-update) | async-done | bytes 2097168 | tf_op jit(solution)/shard_map/psum | solution.py:90
  238.5 2.0 fusion.25
  240.5 10.1 %psum.30 = f32[512,8]{0,1:T(8,128)S(1)} all-reduce(f32[512,8]{0,1:T(8,128)S(1)} %bitcast.101), channel_id=1, replica_groups=mesh['cols'=8,'rows'=4] {'rows'}, use_global_device_ids=true, to_apply=%region_7.0 | all-reduce | flops 4096 | bytes 32768 | tf_op jit(solution)/shard_map/psum | solution.py:90
  250.6 38.7 %psum.31 = f32[512,8]{0,1:T(8,128)S(1)} all-reduce(f32[512,8]{0,1:T(8,128)S(1)} %psum.30), channel_id=1, replica_groups=mesh['cols'=8,'rows'=4] {'cols'}, use_global_device_ids=true, to_apply=%region_8.0 | all-reduce | flops 4096 | bytes 32768 | tf_op jit(solution)/shard_map/psum | solution.py:90
  289.5 55.5 %all-reduce.5.cloned.1.call-done = f32[512,1024]{1,0:T(8,128)} async-done(((f32[512,1024]{1,0:T(8,128)}), f32[512,1024]{1,0:T(8,128)}) %all-reduce.5.cloned.1.call-update) | async-done | bytes 2097168 | tf_op jit(solution)/shard_map/psum | solution.py:90
  345.1 1.5 fusion.61
  (52 shorter events, 2.5 us)
Async XLA Ops:
  6.5 127.3 %copy-start = (bf16[1024,1024]{1,0:T(8,128)(2,1)S(1)}, bf16[1024,1024]{1,0:T(8,128)(2,1)}, u32[]{:S(2)}) copy-start(bf16[1024,1024]{1,0:T(8,128)(2,1)} %param.11) | copy-start | bytes 6291460
  6.5 21.4 %copy-start.1 = (bf16[3,256,512]{2,1,0:T(8,128)(2,1)S(1)}, bf16[3,256,512]{2,1,0:T(8,128)(2,1)}, u32[]{:S(2)}) copy-start(bf16[3,256,512]{2,1,0:T(8,128)(2,1)} %param.7) | copy-start | bytes 2359300
  6.5 232.0 %all-reduce.3.cloned.1.call-start = ((), (), s32[]{:S(2)}) async-start(), calls=%async_computation | async-start | bytes 4194304 | tf_op jit(solution)/shard_map/psum | solution.py:90
  7.8 9.1 %collective-permute-start = (bf16[3,256,1]{2,1,0:T(8,128)(2,1)S(1)}, bf16[3,256,1]{2,1,0:T(8,128)(2,1)S(1)}, u32[]{:S(2)}, u32[]{:S(2)}) collective-permute-start(bf16[3,256,1]{2,1,0:T(8,128)(2,1)S(1)} %get-tuple-element.13), channel_id=1, source_target_pairs={{0,4},{4,8},{8,12},{12,16},{16,20},{20,24},{24,28},{1,5},{5,9},{9,... | collective-permute-start | bytes 4616 | tf_op jit(solution)/shard_map/ppermute | solution.py:17
  12.7 8.3 %collective-permute-start.1 = (bf16[3,256,1]{2,1,0:T(8,128)(2,1)S(1)}, bf16[3,256,1]{2,1,0:T(8,128)(2,1)S(1)}, u32[]{:S(2)}, u32[]{:S(2)}) collective-permute-start(bf16[3,256,1]{2,1,0:T(8,128)(2,1)S(1)} %get-tuple-element.14), channel_id=1, source_target_pairs={{4,0},{8,4},{12,8},{16,12},{20,16},{24,20},{28,24},{5,1},{9,5},{13... | collective-permute-start | bytes 4616 | tf_op jit(solution)/shard_map/ppermute | solution.py:18
  21.8 2.6 collective-permute-start.2
  23.1 4.8 %collective-permute-start.3 = (bf16[3,1,514]{2,1,0:T(2,128)(2,1)S(1)}, bf16[3,1,514]{2,1,0:T(2,128)(2,1)S(1)}, u32[]{:S(2)}, u32[]{:S(2)}) collective-permute-start(bf16[3,1,514]{2,1,0:T(2,128)(2,1)S(1)} %get-tuple-element.10), channel_id=1, source_target_pairs={{1,0},{2,1},{3,2},{5,4},{6,5},{7,6},{9,8},{10,9},{11,10},{13,12},{... | collective-permute-start | bytes 9260 | tf_op jit(solution)/shard_map/ppermute | solution.py:18
  51.2 2.1 copy-start.4
  51.2 2.1 copy-start.5
  79.0 5.9 %collective-permute-start.4 = (bf16[64,64,1]{0,1,2:T(8,128)(2,1)S(1)}, bf16[64,64,1]{0,1,2:T(8,128)(2,1)S(1)}, u32[]{:S(2)}, u32[]{:S(2)}) collective-permute-start(bf16[64,64,1]{0,1,2:T(8,128)(2,1)S(1)} %get-tuple-element.7), channel_id=1, source_target_pairs={{0,4},{4,8},{8,12},{12,16},{16,20},{20,24},{24,28},{1,5},{5,9},{9,... | collective-permute-start | bytes 24584 | tf_op jit(solution)/shard_map/ppermute | solution.py:17
  83.5 6.1 %collective-permute-start.5 = (bf16[64,64,1]{0,1,2:T(8,128)(2,1)S(1)}, bf16[64,64,1]{0,1,2:T(8,128)(2,1)S(1)}, u32[]{:S(2)}, u32[]{:S(2)}) collective-permute-start(bf16[64,64,1]{0,1,2:T(8,128)(2,1)S(1)} %get-tuple-element.8), channel_id=1, source_target_pairs={{4,0},{8,4},{12,8},{16,12},{20,16},{24,20},{28,24},{5,1},{9,5},{13... | collective-permute-start | bytes 24584 | tf_op jit(solution)/shard_map/ppermute | solution.py:18
  89.7 4.6 %collective-permute-start.6 = (bf16[64,1,130]{0,1,2:T(2,128)(2,1)S(1)}, bf16[64,1,130]{0,1,2:T(2,128)(2,1)S(1)}, u32[]{:S(2)}, u32[]{:S(2)}) collective-permute-start(bf16[64,1,130]{0,1,2:T(2,128)(2,1)S(1)} %get-tuple-element.5), channel_id=1, source_target_pairs={{0,1},{1,2},{2,3},{4,5},{5,6},{6,7},{8,9},{9,10},{10,11},{12,13},{... | collective-permute-start | bytes 49928 | tf_op jit(solution)/shard_map/ppermute | solution.py:17
  92.9 3.8 %collective-permute-start.7 = (bf16[64,1,130]{0,1,2:T(2,128)(2,1)S(1)}, bf16[64,1,130]{0,1,2:T(2,128)(2,1)S(1)}, u32[]{:S(2)}, u32[]{:S(2)}) collective-permute-start(bf16[64,1,130]{0,1,2:T(2,128)(2,1)S(1)} %get-tuple-element.6), channel_id=1, source_target_pairs={{1,0},{2,1},{3,2},{5,4},{6,5},{7,6},{9,8},{10,9},{11,10},{13,12},{... | collective-permute-start | bytes 49928 | tf_op jit(solution)/shard_map/ppermute | solution.py:18
  108.9 6.4 %copy-start.3 = (bf16[6,6,64,256]{3,2,1,0:T(8,128)(2,1)S(1)}, bf16[6,6,64,256]{3,2,1,0:T(8,128)(2,1)}, u32[]{:S(2)}) copy-start(bf16[6,6,64,256]{3,2,1,0:T(8,128)(2,1)} %param.9) | copy-start | bytes 3538948
  108.9 6.4 %copy-start.6 = (pred[8,5]{0,1:T(8,128)(4,1)S(1)}, pred[8,5]{0,1:T(8,128)(4,1)}, u32[]{:S(2)}) copy-start(pred[8,5]{0,1:T(8,128)(4,1)} %constant.54) | copy-start | bytes 124
  113.8 17.2 %slice-start = ((s8[4718592]{0:T(1024)(128)(4,1)}), s8[4194304]{0:T(1024)(128)(4,1)S(1)}, s32[]{:S(2)}) async-start(s8[4718592]{0:T(1024)(128)(4,1)} %bitcast.102), calls=%async_computation.2 | async-start | bytes 8388608
  115.3 15.8 %slice-start.1 = ((s8[4718592]{0:T(1024)(128)(4,1)}), s8[524288]{0:T(1024)(128)(4,1)S(1)}, s32[]{:S(2)}) async-start(s8[4718592]{0:T(1024)(128)(4,1)} %bitcast.102), calls=%async_computation.3 | async-start | bytes 1048576
  118.5 12.6 %copy-start.7 = (pred[8,3]{0,1:T(4,128)(4,1)S(1)}, pred[8,3]{0,1:T(4,128)(4,1)}, u32[]{:S(2)}) copy-start(pred[8,3]{0,1:T(4,128)(4,1)} %constant.53) | copy-start | bytes 76
  118.7 5.7 %collective-permute-start.8 = (bf16[1,32,256]{2,0,1:T(2,128)(2,1)S(1)}, bf16[1,32,256]{2,0,1:T(2,128)(2,1)S(1)}, u32[]{:S(2)}, u32[]{:S(2)}) collective-permute-start(bf16[1,32,256]{2,0,1:T(2,128)(2,1)S(1)} %slice.52), channel_id=1, source_target_pairs={{0,1},{1,2},{2,3},{4,5},{5,6},{6,7},{8,9},{9,10},{10,11},{12,13},{... | collective-permute-start | bytes 49160 | tf_op jit(solution)/shard_map/ppermute | solution.py:26
  124.4 6.2 %collective-permute-start.9 = (bf16[17,1,256]{2,0,1:T(8,128)(2,1)S(1)}, bf16[17,1,256]{2,0,1:T(8,128)(2,1)S(1)}, u32[]{:S(2)}, u32[]{:S(2)}) collective-permute-start(bf16[17,1,256]{2,0,1:T(8,128)(2,1)S(1)} %pad_maximum_fusion.3), channel_id=1, source_target_pairs={{0,4},{4,8},{8,12},{12,16},{16,20},{20,24},{24,28},{1,5},{5,9},{9,... | collective-permute-start | bytes 26120 | tf_op jit(solution)/shard_map/ppermute | solution.py:26
  133.4 1.2 copy-start.2
  187.2 157.8 %all-reduce.5.cloned.1.call-start = ((), (), s32[]{:S(2)}) async-start(), calls=%async_computation.1 | async-start | bytes 4194304 | tf_op jit(solution)/shard_map/psum | solution.py:90
Sparse Core Ops, SparseCore 0:
  187.3 51.1 all-reduce.2
  242.6 102.3 all-reduce.4
